TPU v7x, 32 devices: a whole 2x2x4 slice. The times are simulated.
32 devices in a mesh: group: 2 (over x), expert: 16 (over z, y, core).
Axes of the slice: x: 2, y: 2, z: 4, core: 2. Of those that a mesh axis runs over, the one named last changes fastest.
Arguments:
- tokens: bfloat16 [128, 7168], P(('group', 'expert')), parts along dimension 0, may hold values from -6 to 6
- expert_ids: int32 [128, 2], P(('group', 'expert')), parts along dimension 0, may hold values from 0 to 1, all different within a row; in each aligned block of 4 rows (0 to 3, 4 to 7, ...) at most 4 rows name the same one
- gate_codes: int32 [128, 2], P(('group', 'expert')), parts along dimension 0, may hold values from 1 to 65535
- gate_weight: bfloat16 [16, 7168, 256], P('expert'), may hold values from -0.0625 to 0.0625
- up_weight: bfloat16 [16, 7168, 256], P('expert'), may hold values from -0.0625 to 0.0625
- down_weight: bfloat16 [16, 256, 7168], P('expert'), may hold values from -0.125 to 0.125
- target_basis: bfloat16 [7168, 512], P('expert'), may hold values from -0.0625 to 0.0625
Outputs:
- targets: bfloat16 [128, 512], P(('group', 'expert')), parts along dimension 0
There are 2 independent parts, one for each index of `group`. A program takes and returns all parts, laid end to end along the dimension named above; an argument that names none is the same for every part. Nothing has to cross between parts.
Inputs may be any that keep to these rules, and one draw needn't show every extreme that they name: `expert_ids`: each row names 2 different experts; among the 4 rows of one device no expert is named more than 4 times, a bound that some block reaches.
All inputs are finite; a program needn't handle non-finite values.
Results may differ from a plain program's by a relative error of at most 0.0057.
Values may be sent and summed in bfloat16 or wider, within the bound.
No kernel may reach another device: no remote copies, remote signals or barrier semaphores. Data moves between devices by JAX's collectives and lax.ppermute only.
A program may use at most 128 MiB of HBM per device.

v0:
```python
import jax
import jax.numpy as jnp
from jax import lax
from jax.sharding import PartitionSpec as P

SLICES = 8


def run_expert(received, gate_weight, up_weight, down_weight):
    sources, slots, feature_width = received.shape
    row_block = received.reshape(sources * slots, feature_width)
    gate_act = jnp.dot(row_block, gate_weight[0], preferred_element_type=jnp.float32)
    up_act = jnp.dot(row_block, up_weight[0], preferred_element_type=jnp.float32)
    hidden = (jax.nn.silu(gate_act) * up_act).astype(jnp.bfloat16)
    expert_part = jnp.dot(hidden, down_weight[0], preferred_element_type=jnp.float32).astype(
        jnp.bfloat16
    )
    return expert_part.reshape(sources, slots, feature_width)


def shards(tokens, expert_ids, gate_codes, gate_weight, up_weight, down_weight, target_basis):
    token_count, feature_width = tokens.shape
    pick_count = expert_ids.shape[1]
    owner_count = lax.axis_size("expert")
    expert_count = owner_count // SLICES
    capacity = min(token_count, max(2, 5 * token_count * pick_count // (4 * expert_count)))
    rank_width = target_basis.shape[1]
    flat_ids = expert_ids.reshape(-1)
    onehot = (flat_ids[:, None] == jnp.arange(expert_count, dtype=jnp.int32)[None, :]).astype(
        jnp.int32
    )
    before = jnp.cumsum(onehot, axis=0) - onehot
    slot_rank = jnp.sum(before * onehot, axis=1)
    slot_index = flat_ids * capacity + slot_rank
    row_token = jnp.arange(token_count * pick_count, dtype=jnp.int32) // pick_count
    slot_table = (
        jnp.full((expert_count * capacity,), token_count, jnp.int32).at[slot_index].set(row_token)
    )
    padded = jnp.concatenate([tokens, jnp.zeros((1, feature_width), tokens.dtype)], axis=0)
    per_expert_rows = padded[slot_table].reshape(expert_count, 1, capacity, feature_width)
    outgoing = jnp.broadcast_to(per_expert_rows, (expert_count, SLICES, capacity, feature_width))
    outgoing = outgoing.reshape(owner_count, capacity, feature_width)
    full_basis = lax.all_gather(target_basis, "expert", axis=0, tiled=True)
    expert_part = run_expert(
        lax.all_to_all(outgoing, "expert", split_axis=0, concat_axis=0, tiled=True),
        gate_weight,
        up_weight,
        down_weight,
    )
    result = jnp.einsum("skd,dr->skr", expert_part, full_basis, preferred_element_type=jnp.float32)
    returned = lax.all_to_all(result, "expert", split_axis=0, concat_axis=0, tiled=True)
    summed = jnp.sum(returned.reshape(expert_count, SLICES, capacity, rank_width), axis=1)
    projected = summed.reshape(expert_count * capacity, rank_width)[slot_index]
    codes_float = gate_codes.astype(jnp.float32)
    weights = 2.5 * codes_float / jnp.sum(codes_float, axis=1, keepdims=True)
    projected = projected.reshape(token_count, pick_count, rank_width)
    return jnp.sum(weights[:, :, None] * projected, axis=1).astype(jnp.bfloat16)


def solution(mesh):
    in_specs = (
        P(("group", "expert"), None),
        P(("group", "expert"), None),
        P(("group", "expert"), None),
        P("expert", None, None),
        P("expert", None, None),
        P("expert", None, None),
        P("expert", None),
    )
    out_specs = P(("group", "expert"), None)
    return jax.shard_map(shards, mesh=mesh, in_specs=in_specs, out_specs=out_specs, check_vma=False)
```

profile of v0, /device:TPU:0, one launch (start us, length us, event | category | flops | bytes accessed | tf_op | source)
XLA Modules:
  0.0 121.8 jit_solution(8186890199680378276)
XLA Ops:
  6.5 0.0 copy-start
  6.5 0.0 all-gather.2.cloned.1.call-start
  6.5 0.7 all-gather.2.cloned.1.call-update
  7.3 0.8 copy.25
  8.0 0.1 eq.15
  8.1 0.7 broadcast_multiply_fusion
  8.8 0.1 copy.24
  8.9 0.1 mul.37
  9.0 0.2 reduce_window_sum.11
  9.2 0.8 concatenate.3
  10.1 0.6 scatter_custom_fusion
  10.7 0.6 gather_fusion
  11.3 0.1 broadcast_in_dim.7
  11.4 1.2 broadcast_in_dim.8
  12.5 7.4 %all-to-all-start = ((bf16[16,4,7168]{2,1,0:T(4,128)(2,1)}), bf16[16,4,7168]{2,1,0:T(4,128)(2,1)S(1)}, u32[]{:S(2)}, u32[]{:S(2)}) async-start(bf16[16,4,7168]{2,1,0:T(4,128)(2,1)} %bitcast.2), calls=%async_computation | async-start | bytes 1835008 | tf_op jit(solution)/shard_map/all_to_all | solution.py:45
  19.9 0.0 copy-done
  20.0 35.1 %all-to-all-done = bf16[16,4,7168]{2,1,0:T(4,128)(2,1)S(1)} async-done(((bf16[16,4,7168]{2,1,0:T(4,128)(2,1)}), bf16[16,4,7168]{2,1,0:T(4,128)(2,1)S(1)}, u32[]{:S(2)}, u32[]{:S(2)}) %all-to-all-start) | async-done | bytes 917536 | tf_op jit(solution)/shard_map/all_to_all | solution.py:45
  55.1 0.2 reshape.53
  55.3 2.8 %fusion.5 = f32[64,256]{1,0:T(8,128)S(1)} fusion(bf16[64,7168]{1,0:T(8,128)(2,1)S(1)} %reshape.53, bf16[1,7168,256]{2,1,0:T(8,128)(2,1)} %param.10), kind=kOutput, calls=%fused_computation.9 | convolution fusion | flops 234881024 | bytes 4653056 | tf_op jit(solution)/shard_map/dot_general | solution.py:12
  58.0 5.5 %convolution_convert_fusion = bf16[64,7168]{1,0:T(8,128)(2,1)S(1)} fusion(bf16[1,256,7168]{2,1,0:T(8,128)(2,1)} %param.12, bf16[64,7168]{1,0:T(8,128)(2,1)S(1)} %reshape.53, bf16[1,7168,256]{2,1,0:T(8,128)(2,1)} %param.11, f32[64,256]{1,0:T(8,128)S(1)} %fusion.5), kind=kOutput, calls=%fused_computation.3 | convolution fusion | flops 470319104 | bytes 9240576 | tf_op jit(solution)/shard_map/dot_general | solution.py:15
  63.5 0.3 reshape.54
  63.8 33.4 %all-gather.2.cloned.1.call-done = bf16[7168,512]{1,0:T(8,128)(2,1)} async-done(((bf16[448,512]{1,0:T(8,128)(2,1)}), bf16[7168,512]{1,0:T(8,128)(2,1)}) %all-gather.2.cloned.1.call-update) | async-done | bytes 7340048 | tf_op jit(solution)/shard_map/all_gather | solution.py:43
  97.3 4.2 %fusion = f32[16,4,512]{2,0,1:T(8,128)S(1)} fusion(bf16[7168,512]{1,0:T(8,128)(2,1)} %all-gather.2.cloned.1.call-done, bf16[16,4,7168]{2,1,0:T(4,128)(2,1)S(1)} %reshape.54), kind=kOutput, calls=%fused_computation.4 | convolution fusion | flops 469762048 | bytes 8388608 | tf_op jit(solution)/shard_map/skd,dr->skr/dot_general | solution.py:50
  101.5 0.7 copy.27
  102.2 3.5 %all-to-all-start.1 = ((f32[16,4,512]{2,1,0:T(4,128)}), f32[16,4,512]{2,1,0:T(4,128)S(1)}, u32[]{:S(2)}, u32[]{:S(2)}) async-start(f32[16,4,512]{2,1,0:T(4,128)} %copy.27), calls=%async_computation.1 | async-start | bytes 262144 | tf_op jit(solution)/shard_map/all_to_all | solution.py:51
  105.8 0.1 copy.23
  105.9 7.8 %all-to-all-done.1 = f32[16,4,512]{2,1,0:T(4,128)S(1)} async-done(((f32[16,4,512]{2,1,0:T(4,128)}), f32[16,4,512]{2,1,0:T(4,128)S(1)}, u32[]{:S(2)}, u32[]{:S(2)}) %all-to-all-start.1) | async-done | bytes 131104 | tf_op jit(solution)/shard_map/all_to_all | solution.py:51
  113.7 0.6 gather_fusion.1
  114.2 0.7 multiply_reduce_fusion
  (12 shorter events, 0.1 us)
Async XLA Ops:
  6.5 13.4 %copy-start = (s32[4,2]{0,1:T(2,128)S(1)}, s32[4,2]{0,1:T(2,128)}, u32[]{:S(2)}) copy-start(s32[4,2]{0,1:T(2,128)} %param.9) | copy-start | bytes 100
  6.5 90.7 %all-gather.2.cloned.1.call-start = ((), (), s32[]{:S(2)}) async-start(), calls=%async_computation.2 | async-start | bytes 7798784 | tf_op jit(solution)/shard_map/all_gather | solution.py:43
  12.5 42.5 %all-to-all-start = ((bf16[16,4,7168]{2,1,0:T(4,128)(2,1)}), bf16[16,4,7168]{2,1,0:T(4,128)(2,1)S(1)}, u32[]{:S(2)}, u32[]{:S(2)}) async-start(bf16[16,4,7168]{2,1,0:T(4,128)(2,1)} %bitcast.2), calls=%async_computation | async-start | bytes 1835008 | tf_op jit(solution)/shard_map/all_to_all | solution.py:45
  102.2 11.4 %all-to-all-start.1 = ((f32[16,4,512]{2,1,0:T(4,128)}), f32[16,4,512]{2,1,0:T(4,128)S(1)}, u32[]{:S(2)}, u32[]{:S(2)}) async-start(f32[16,4,512]{2,1,0:T(4,128)} %copy.27), calls=%async_computation.1 | async-start | bytes 262144 | tf_op jit(solution)/shard_map/all_to_all | solution.py:51
Sparse Core Ops, SparseCore 0:
  9.6 87.5 all-gather.1
where the time goes:
time: 122 us
  waiting for transfers between devices  77 us (63%)
  between operations  13.5 us (11%)
  matrix products  12.4 us (10%)
  starting transfers between devices  10.9 us (9%)
  local copies, waits for them, and re-layouts  6.25 us (5%)
  other arithmetic  1.66 us (1%)
    all_to_all x1, waiting for transfers between devices, shards(): lax.all_to_all(outgoing, 'expert', split_axis=0, concat_axis=0, tiled=True)  35.1 us
    all_gather x1, waiting for transfers between devices, shards(): full_basis = lax.all_gather(target_basis, 'expert', axis=0, tiled=True)  33.4 us
    all_to_all x1, waiting for transfers between devices, shards(): lax.all_to_all(result, 'expert', split_axis=0, concat_axis=0, tiled=True)  7.76 us
    all_to_all x1, starting transfers between devices, shards(): lax.all_to_all(outgoing, 'expert', split_axis=0, concat_axis=0, tiled=True)  7.41 us
    dot_general x1, matrix products, run_expert(): jnp.dot(hidden, down_weight[0], preferred_element_type=jnp.float32)  5.45 us
    dot_general x1, matrix products, shards(): jnp.einsum('skd,dr->skr', expert_part, full_basis, preferred_element_type...  4.23 us
    all_to_all x1, starting transfers between devices, shards(): lax.all_to_all(result, 'expert', split_axis=0, concat_axis=0, tiled=True)  3.51 us
    dot_general x1, matrix products, run_expert(): jnp.dot(row_block, gate_weight[0], preferred_element_type=jnp.float32)  2.76 us
  transfers between devices with their start and end apart: 3, of which 3 were waited for; matrix products, arithmetic and copies ran while one was open for 12% of the time, Pallas kernels for 0%

commit v1 on v0

--- a/solution.py
+++ b/solution.py
@@ -40,7 +40,9 @@
     per_expert_rows = padded[slot_table].reshape(expert_count, 1, capacity, feature_width)
     outgoing = jnp.broadcast_to(per_expert_rows, (expert_count, SLICES, capacity, feature_width))
     outgoing = outgoing.reshape(owner_count, capacity, feature_width)
-    full_basis = lax.all_gather(target_basis, "expert", axis=0, tiled=True)
+    full_basis = jnp.concatenate(
+        lax.all_to_all(jnp.stack([target_basis] * lax.axis_size("expert")), "expert", 0, 0), axis=0
+    )
     expert_part = run_expert(
         lax.all_to_all(outgoing, "expert", split_axis=0, concat_axis=0, tiled=True),
         gate_weight,

time: 122 us -> 222 us (1.82)
  waiting for transfers between devices: 77 us -> 131 us
  blocking collectives: 0 us -> 29.6 us
  starting transfers between devices: 10.9 us -> 37.3 us
  between operations: 13.5 us -> 0.12 us
  local copies, waits for them, and re-layouts: 6.25 us -> 9.07 us
    all_to_all x1, waiting for transfers between devices: 35.1 us -> 123 us  [shards(): lax.all_to_all(jnp.stack([target_basis] * lax.axis_size('expert')), 'expe...]
    all_gather x1 -> x0, waiting for transfers between devices: 33.4 us -> none  [shards(): full_basis = lax.all_gather(target_basis, 'expert', axis=0, tiled=True)]
    all_to_all x0 -> x1, blocking collectives: none -> 29.6 us  [shards(): lax.all_to_all(outgoing, 'expert', split_axis=0, concat_axis=0, tiled=True)]
    all_to_all x1, starting transfers between devices: 3.51 us -> 32.5 us  [shards(): lax.all_to_all(result, 'expert', split_axis=0, concat_axis=0, tiled=True)]
    another operation x0 -> x1, local copies, waits for them, and re-layouts: none -> 3.74 us  [shards(): jnp.stack([target_basis] * lax.axis_size('expert'))]
    all_to_all x1, starting transfers between devices: 7.41 us -> 4.82 us  [shards(): lax.all_to_all(jnp.stack([target_basis] * lax.axis_size('expert')), 'expe...]
  transfers between devices with their start and end apart: 3 -> 2, of which waited for: 3 -> 2; matrix products, arithmetic and copies ran while one was open for 12% -> 4% of each run, Pallas kernels for 0% -> 0%
where the time goes in v1:
time: 222 us
  waiting for transfers between devices  131 us (59%)
  starting transfers between devices  37.3 us (17%)
  blocking collectives  29.6 us (13%)
  matrix products  12.4 us (6%)
  local copies, waits for them, and re-layouts  9.07 us (4%)
    all_to_all x1, waiting for transfers between devices, shards(): lax.all_to_all(jnp.stack([target_basis] * lax.axis_size('expert')), 'expe...  123 us
    all_to_all x1, starting transfers between devices, shards(): lax.all_to_all(result, 'expert', split_axis=0, concat_axis=0, tiled=True)  32.5 us
    all_to_all x1, blocking collectives, shards(): lax.all_to_all(outgoing, 'expert', split_axis=0, concat_axis=0, tiled=True)  29.6 us
    all_to_all x1, waiting for transfers between devices, shards(): lax.all_to_all(result, 'expert', split_axis=0, concat_axis=0, tiled=True)  7.79 us
    dot_general x1, matrix products, run_expert(): jnp.dot(hidden, down_weight[0], preferred_element_type=jnp.float32)  5.45 us
    all_to_all x1, starting transfers between devices, shards(): lax.all_to_all(jnp.stack([target_basis] * lax.axis_size('expert')), 'expe...  4.82 us
  transfers between devices with their start and end apart: 2, of which 2 were waited for; matrix products, arithmetic and copies ran while one was open for 4% of the time, Pallas kernels for 0%

profile of v1, /device:TPU:0, one launch (start us, length us, event | category | flops | bytes accessed | tf_op | source)
XLA Modules:
  0.0 221.5 jit_solution(3737642472663608270)
XLA Ops:
  0.0 0.0 copy-start
  0.0 0.7 broadcast_multiply_fusion
  0.7 0.8 copy.25
  1.5 0.1 copy.24
  1.6 0.1 mul.37
  1.7 0.1 eq.15
  1.8 0.2 reduce_window_sum.11
  2.0 0.6 scatter_custom_fusion
  2.6 0.8 concatenate.3
  3.5 0.6 gather_fusion
  4.1 0.1 broadcast_in_dim.7
  4.2 0.2 broadcast_in_dim.8
  4.4 29.6 %all_to_all.15 = bf16[16,4,7168]{2,1,0:T(4,128)(2,1)S(1)} all-to-all(bf16[16,4,7168]{2,1,0:T(4,128)(2,1)S(1)} %bitcast.30), channel_id=1, replica_groups=mesh['group'=2,'expert'=16] {'expert'}, dimensions={0} | all-to-all | bytes 1835008 | tf_op jit(solution)/shard_map/all_to_all | solution.py:47
  34.0 0.0 copy-done
  34.0 3.7 %stack.2 = bf16[16,448,512]{2,1,0:T(8,128)(2,1)} broadcast(bf16[448,512]{1,0:T(8,128)(2,1)S(1)} %copy-done), dimensions={1,2} | broadcast | bytes 7798784 | tf_op jit(solution)/shard_map/stack | solution.py:44
  37.8 0.0 copy-start.1
  37.8 4.8 %all-to-all-start.1 = ((bf16[16,448,512]{2,1,0:T(8,128)(2,1)}), bf16[16,448,512]{2,1,0:T(8,128)(2,1)}, u32[]{:S(2)}, u32[]{:S(2)}) async-start(bf16[16,448,512]{2,1,0:T(8,128)(2,1)} %stack.2), calls=%async_computation.1 | async-start | bytes 14680064 | tf_op jit(solution)/shard_map/all_to_all | solution.py:44
  42.6 0.0 copy-done.1
  42.6 0.2 reshape.58
  42.8 2.8 %fusion.3 = f32[64,256]{1,0:T(8,128)S(1)} fusion(bf16[64,7168]{1,0:T(8,128)(2,1)S(1)} %reshape.58, bf16[1,7168,256]{2,1,0:T(8,128)(2,1)} %param.10), kind=kOutput, calls=%fused_computation.7 | convolution fusion | flops 234881024 | bytes 4653056 | tf_op jit(solution)/shard_map/dot_general | solution.py:12
  45.6 5.5 %convolution_convert_fusion = bf16[64,7168]{1,0:T(8,128)(2,1)S(1)} fusion(bf16[1,256,7168]{2,1,0:T(8,128)(2,1)} %param.12, bf16[64,7168]{1,0:T(8,128)(2,1)S(1)} %reshape.58, bf16[1,7168,256]{2,1,0:T(8,128)(2,1)} %param.11, f32[64,256]{1,0:T(8,128)S(1)} %fusion.3), kind=kOutput, calls=%fused_computation.3 | convolution fusion | flops 470319104 | bytes 9240576 | tf_op jit(solution)/shard_map/dot_general | solution.py:15
  51.0 0.3 reshape.59
  51.4 123.5 %all-to-all-done.1 = bf16[16,448,512]{2,1,0:T(8,128)(2,1)} async-done(((bf16[16,448,512]{2,1,0:T(8,128)(2,1)}), bf16[16,448,512]{2,1,0:T(8,128)(2,1)}, u32[]{:S(2)}, u32[]{:S(2)}) %all-to-all-start.1) | async-done | bytes 7340064 | tf_op jit(solution)/shard_map/all_to_all | solution.py:44
  174.8 4.2 %fusion.11 = f32[16,4,512]{2,0,1:T(8,128)S(1)} fusion(bf16[7168,512,1]{1,0,2:T(8,128)(2,1)} %bitcast.7, bf16[16,4,7168]{2,1,0:T(4,128)(2,1)S(1)} %reshape.59), kind=kOutput, calls=%fused_computation.11 | convolution fusion | flops 469762048 | bytes 8388608 | tf_op jit(solution)/shard_map/skd,dr->skr/dot_general | solution.py:52
  179.1 0.7 copy.27
  179.8 32.5 %all-to-all-start.2 = ((f32[16,4,512]{2,1,0:T(4,128)}), f32[16,4,512]{2,1,0:T(4,128)S(1)}, u32[]{:S(2)}, u32[]{:S(2)}) async-start(f32[16,4,512]{2,1,0:T(4,128)} %copy.27), calls=%async_computation.2 | async-start | bytes 262144 | tf_op jit(solution)/shard_map/all_to_all | solution.py:53
  212.3 0.1 copy.23
  212.4 7.8 %all-to-all-done.2 = f32[16,4,512]{2,1,0:T(4,128)S(1)} async-done(((f32[16,4,512]{2,1,0:T(4,128)}), f32[16,4,512]{2,1,0:T(4,128)S(1)}, u32[]{:S(2)}, u32[]{:S(2)}) %all-to-all-start.2) | async-done | bytes 131104 | tf_op jit(solution)/shard_map/all_to_all | solution.py:53
  220.2 0.6 gather_fusion.1
  220.8 0.7 multiply_reduce_fusion
  (12 shorter events, 0.1 us)
Async XLA Ops:
  0.0 34.0 %copy-start = (bf16[448,512]{1,0:T(8,128)(2,1)S(1)}, bf16[448,512]{1,0:T(8,128)(2,1)}, u32[]{:S(2)}) copy-start(bf16[448,512]{1,0:T(8,128)(2,1)} %param.13) | copy-start | bytes 1376260
  37.8 4.8 %copy-start.1 = (s32[4,2]{0,1:T(2,128)S(1)}, s32[4,2]{0,1:T(2,128)}, u32[]{:S(2)}) copy-start(s32[4,2]{0,1:T(2,128)} %param.9) | copy-start | bytes 100
  37.8 137.1 %all-to-all-start.1 = ((bf16[16,448,512]{2,1,0:T(8,128)(2,1)}), bf16[16,448,512]{2,1,0:T(8,128)(2,1)}, u32[]{:S(2)}, u32[]{:S(2)}) async-start(bf16[16,448,512]{2,1,0:T(8,128)(2,1)} %stack.2), calls=%async_computation.1 | async-start | bytes 14680064 | tf_op jit(solution)/shard_map/all_to_all | solution.py:44
  179.8 40.4 %all-to-all-start.2 = ((f32[16,4,512]{2,1,0:T(4,128)}), f32[16,4,512]{2,1,0:T(4,128)S(1)}, u32[]{:S(2)}, u32[]{:S(2)}) async-start(f32[16,4,512]{2,1,0:T(4,128)} %copy.27), calls=%async_computation.2 | async-start | bytes 262144 | tf_op jit(solution)/shard_map/all_to_all | solution.py:53
